TPU v7x, 32 devices: a whole 2x2x4 slice. The times are simulated.
32 devices in a mesh: scen: 4 (over y, x), col: 8 (over z, core).
Axes of the slice: x: 2, y: 2, z: 4, core: 2. Of those that a mesh axis runs over, the one named last changes fastest.
Arguments:
- border: float32 [8, 2048, 16384], P('scen', None, 'col'), may hold values from -0.046875 to 0.046875
- pattern: int32 [8, 16, 128], P('scen', None, 'col'), may hold values 0 or 1
- slack: float32 [8, 2048], P('scen'), may hold values from 0.5 to 2
- first_diag: float32 [16384], P('col'), may hold values from 0.25 to 1.75
- rhs: float32 [16384, 256], P('col'), may hold values from -6 to 6
- scen_rhs: float32 [8, 2048, 256], P('scen', 'col'), may hold values from -6 to 6
Outputs:
- reduced: float32 [8, 2048, 256], P('col', 'scen')
- directions: float32 [8, 2048, 256], P('scen', 'col')
All inputs are finite; a program needn't handle non-finite values. No bound on the sum of `pattern` on one device may be relied on, other than what follows from the above.
Results may differ from a plain program's by a relative error of at most 0.0001.
Values sent between devices are 32-bit elements; how exact they have to be, the bound alone decides.
A program may use at most 192 MiB of HBM per device.

v0:
```python
import jax
import jax.numpy as jnp
from jax import lax
from jax.sharding import PartitionSpec as P

PW = 512


def add_diagonal(rows, row_start, first_diag, col_index, pivot_width):
    row_count = rows.shape[0]
    local_rows = row_start + jnp.arange(row_count, dtype=jnp.int32)
    diag_rows = lax.dynamic_slice_in_dim(first_diag, row_start, row_count)
    panel_cols = jnp.arange(rows.shape[1], dtype=jnp.int32)
    on_diag = (local_rows[:, None] < pivot_width) & (
        panel_cols[None, :] == col_index * pivot_width + local_rows[:, None]
    )
    return rows + jnp.where(on_diag, diag_rows[:, None], jnp.zeros_like(rows))


def per_device(border, pattern, slack, first_diag, rhs, scen_rhs):
    col_count = lax.axis_size("col")
    col_index = lax.axis_index("col")
    scen_index = lax.axis_index("scen")
    scen_local, row_total, own_width = border.shape
    row_blocks = pattern.shape[1]
    width_blocks = pattern.shape[2]
    pivot_width = PW // col_count
    row_share = row_total // col_count
    own_share = own_width // lax.axis_size("scen")
    weights = pattern.astype(jnp.float32)[:, :, None, :, None]
    masked = border.reshape(
        scen_local, row_blocks, row_total // row_blocks, width_blocks, own_width // width_blocks
    )
    masked = (masked * weights).reshape(scen_local, row_total, own_width)
    own_panel = masked[:, :, :pivot_width]
    flat_masked = masked.reshape(scen_local * row_total, own_width)
    inverse_slack = (1.0 / slack).reshape(scen_local * row_total, 1)
    shard_cols = lax.all_gather(own_panel, "col", axis=2, tiled=True)
    scaled = shard_cols.reshape(scen_local * row_total, shard_cols.shape[2]) * inverse_slack
    schur_term = lax.dot_general(
        flat_masked,
        scaled,
        (((0,), (0,)), ((), ())),
        precision=lax.Precision.HIGHEST,
        preferred_element_type=jnp.float32,
    )
    my_panel = lax.all_to_all(own_panel, "col", split_axis=1, concat_axis=2, tiled=True)
    pivot_summed = schur_term[:pivot_width]
    schur_rows = lax.psum_scatter(schur_term, "scen", scatter_dimension=0, tiled=True)
    pivot_summed = lax.psum(schur_term[:pivot_width], "scen")
    row_start = scen_index * own_share
    row_count = schur_rows.shape[0]
    local_rows = row_start + jnp.arange(row_count, dtype=jnp.int32)
    schur_rows = add_diagonal(schur_rows, row_start, first_diag, col_index, pivot_width)
    pivot_source = add_diagonal(pivot_summed, jnp.int32(0), first_diag, col_index, pivot_width)
    pivot_block, rhs_panel = (
        lax.all_gather(pivot_source, "col", axis=0, tiled=True),
        lax.all_gather(rhs[:pivot_width], "col", axis=0, tiled=True),
    )
    factor = jnp.linalg.cholesky(pivot_block)
    forward = lax.linalg.triangular_solve(factor, rhs_panel, left_side=True, lower=True)
    solved = lax.linalg.triangular_solve(
        factor, forward, left_side=True, lower=True, transpose_a=True
    )
    rhs_rows = lax.dynamic_slice_in_dim(rhs, row_start, row_count)
    reduced = rhs_rows - jnp.dot(
        schur_rows, solved, precision=lax.Precision.HIGHEST, preferred_element_type=jnp.float32
    )
    mine_forward = lax.dynamic_slice_in_dim(forward, col_index * pivot_width, pivot_width)
    padded = jnp.concatenate(
        [mine_forward, jnp.zeros((own_width - pivot_width, forward.shape[1]), jnp.float32)], axis=0
    )
    placed = lax.dynamic_slice_in_dim(padded, row_start, row_count)
    reduced = jnp.where((local_rows < pivot_width)[:, None], placed, reduced)
    slack_rows = lax.dynamic_slice_in_dim(slack, col_index * row_share, row_share, 1)
    moved = jnp.dot(
        my_panel.reshape(scen_local * row_share, my_panel.shape[2]),
        solved,
        precision=lax.Precision.HIGHEST,
        preferred_element_type=jnp.float32,
    )
    moved = moved.reshape(scen_local, row_share, solved.shape[1])
    directions = (scen_rhs - moved) / slack_rows[:, :, None]
    return (reduced[None], directions)


def solution(mesh):
    return jax.shard_map(
        per_device,
        mesh=mesh,
        in_specs=(
            P("scen", None, "col"),
            P("scen", None, "col"),
            P("scen", None),
            P("col"),
            P("col", None),
            P("scen", "col", None),
        ),
        out_specs=(P("col", "scen", None), P("scen", "col", None)),
        check_vma=False,
    )
```

profile of v0, /device:TPU:0, one launch (start us, length us, event | category | flops | bytes accessed | tf_op | source)
XLA Modules:
  0.0 609.0 jit_solution(8212648014695701368)
XLA Ops:
  8.0 11.3 %mul.34 = f32[2,16,128,16,128]{2,1,0,4,3:T(8,128)} broadcast(f32[2,16,16]{1,0,2:T(2,128)S(1)} %copy.22), dimensions={0,1,3} | broadcast | bytes 33556480 | tf_op jit(solution)/shard_map/mul | solution.py:34
  19.3 40.5 %mul.35 = f32[2,2048,2048]{1,0,2:T(2,128)} reshape(f32[2,16,128,16,128]{2,1,0,4,3:T(8,128)} %mul.34) | data formatting | bytes 67108864 | tf_op jit(solution)/shard_map/mul | solution.py:34
  59.8 49.4 %copy.23 = f32[2,2048,2048]{1,0,2:T(2,128)} copy(f32[2,2048,2048]{2,1,0:T(8,128)} %param.6) | data formatting | bytes 67108864 | tf_op args[0]
  109.2 33.3 %mul.36 = f32[2,2048,2048]{1,0,2:T(2,128)} multiply(f32[2,2048,2048]{1,0,2:T(2,128)} %copy.23, f32[2,2048,2048]{1,0,2:T(2,128)} %mul.35) | non-fusion elementwise | flops 8388608 | bytes 100663296 | tf_op jit(solution)/shard_map/mul | solution.py:34
  142.5 2.4 slice.148
  145.0 84.8 %all-gather.3.cloned.1.call-done = f32[2,2048,512]{1,0,2:T(2,128)} async-done(((f32[2,2048,64]{1,0,2:T(2,128)}), f32[2,2048,512]{1,0,2:T(2,128)}) %all-gather.3.cloned.1.call-update) | async-done | bytes 8388624 | tf_op jit(solution)/shard_map/all_gather | solution.py:38
  229.8 4.2 broadcast_multiply_fusion
  234.1 119.1 %fusion.3 = f32[2048,512]{1,0:T(8,128)} fusion(f32[2,2048,512]{1,0,2:T(2,128)S(1)} %bitcast.82, f32[2,2048,2048]{1,0,2:T(2,128)} %mul.36), kind=kOutput, calls=%fused_computation.6 | convolution fusion | flops 51539607552 | bytes 46137344 | tf_op jit(solution)/shard_map/dot_general | solution.py:40
  353.2 1.6 slice.149
  354.9 40.8 %all-reduce.4.cloned.1.call-done = f32[64,512]{1,0:T(8,128)} async-done(((f32[64,512]{1,0:T(8,128)}), f32[64,512]{1,0:T(8,128)}) %all-reduce.4.cloned.1.call-update) | async-done | bytes 131088 | tf_op jit(solution)/shard_map/psum | solution.py:50
  395.7 1.7 select_add_fusion
  398.5 3.1 reshape.114
  401.6 4.6 all-to-all-start
  406.9 42.1 %all_gather.11 = f32[512,256]{1,0:T(8,128)} all-gather(f32[64,256]{1,0:T(8,128)S(1)} %slice-done), channel_id=1, replica_groups=mesh['scen'=4,'col'=8] {'col'}, dimensions={0}, use_global_device_ids=true | all-gather | bytes 589824 | tf_op jit(solution)/shard_map/all_gather | solution.py:58
  449.5 3.1 reduce.24
  452.6 1.5 reshape.115
  454.1 2.1 copy.33
  456.2 1.6 copy.26
  457.8 1.4 fusion.11
  459.2 11.7 %cholesky.104 = f32[128,128]{1,0:T(8,128)S(1)} custom-call(f32[128,128]{1,0:T(8,128)S(1)} %cholesky.266), custom_call_target="Cholesky" | custom-call | tf_op jit(solution)/shard_map/jit(cholesky)/cholesky | solution.py:60
  471.0 9.8 %custom-call.32 = f32[1,128,128]{1,2,0:T(8,128)S(1)} custom-call(f32[1,128,128]{2,1,0:T(8,128)S(1)} %get-tuple-element.29), custom_call_target="InvertDiagBlocksLowerTriangular" | custom-call | tf_op jit(solution)/shard_map/jit(cholesky)/cholesky | solution.py:60
  481.6 11.7 %cholesky.217 = f32[128,128]{1,0:T(8,128)S(1)} custom-call(f32[128,128]{1,0:T(8,128)S(1)} %cholesky.270), custom_call_target="Cholesky" | custom-call | tf_op jit(solution)/shard_map/jit(cholesky)/cholesky | solution.py:60
  493.3 10.2 %custom-call.33 = f32[1,128,128]{1,2,0:T(8,128)S(1)} custom-call(f32[1,128,128]{2,1,0:T(8,128)S(1)} %get-tuple-element.26), custom_call_target="InvertDiagBlocksLowerTriangular" | custom-call | tf_op jit(solution)/shard_map/jit(cholesky)/cholesky | solution.py:60
  504.2 11.7 %cholesky.238 = f32[128,128]{1,0:T(8,128)S(1)} custom-call(f32[128,128]{1,0:T(8,128)S(1)} %cholesky.275), custom_call_target="Cholesky" | custom-call | tf_op jit(solution)/shard_map/jit(cholesky)/cholesky | solution.py:60
  515.9 9.8 %custom-call.34 = f32[1,128,128]{1,2,0:T(8,128)S(1)} custom-call(f32[1,128,128]{2,1,0:T(8,128)S(1)} %get-tuple-element.23), custom_call_target="InvertDiagBlocksLowerTriangular" | custom-call | tf_op jit(solution)/shard_map/jit(cholesky)/cholesky | solution.py:60
  526.4 11.7 %cholesky.255 = f32[128,128]{1,0:T(8,128)S(1)} custom-call(f32[128,128]{1,0:T(8,128)S(1)} %convolution_subtract_fusion.10), custom_call_target="Cholesky" | custom-call | tf_op jit(solution)/shard_map/jit(cholesky)/cholesky | solution.py:60
  542.8 8.2 %while.1 = (s32[]{:T(128)}, f32[512,512]{1,0:T(8,128)S(1)}, s32[4,2]{0,1:T(2,128)S(1)}, f32[4,128,128]{2,1,0:T(8,128)S(1)}, s32[]{:T(128)}) while((s32[]{:T(128)}, f32[512,512]{1,0:T(8,128)S(1)}, s32[4,2]{0,1:T(2,128)S(1)}, f32[4,128,128]{2,1,0:T(8,128)S(1)}, s32[]{:T(128)}) %tuple.31), condition=%wide.while_cond, body=%wide.while_body.sunk | while | flops 2 | bytes 131181 | solution.py:61
  543.6 1.4 bitcast_dynamic-update-slice_fusion.2
  547.6 1.4 bitcast_dynamic-update-slice_fusion.2
  551.0 39.3 %custom-call.35 = f32[4,128,128]{1,2,0:T(8,128)S(1)} custom-call(f32[4,128,128]{2,1,0:T(8,128)S(1)} %get-tuple-element.9), custom_call_target="InvertDiagBlocksLowerTriangular" | custom-call | tf_op jit(solution)/shard_map/triangular_solve | solution.py:61
  594.9 4.0 fusion.10
  598.9 3.4 fusion.9
  (81 shorter events, 17.2 us)
Async XLA Ops:
  7.2 222.6 %all-gather.3.cloned.1.call-start = ((), (), s32[]{:S(2)}) async-start(), calls=%async_computation.2 | async-start | bytes 9437184 | tf_op jit(solution)/shard_map/all_gather | solution.py:38
  109.2 35.8 %copy-start.2 = (f32[2,2048]{1,0:T(2,128)S(1)}, f32[2,2048]{1,0:T(2,128)}, u32[]{:S(2)}) copy-start(f32[2,2048]{1,0:T(2,128)} %param.8) | copy-start | bytes 49156
  144.9 250.8 %all-reduce.4.cloned.1.call-start = ((), (), s32[]{:S(2)}) async-start(), calls=%async_computation.3 | async-start | bytes 262144 | tf_op jit(solution)/shard_map/psum | solution.py:50
  234.1 161.6 %slice-start.1 = ((f32[2048]{0:T(1024)}), f32[64]{0:T(128)S(1)}, s32[]{:S(2)}) async-start(f32[2048]{0:T(1024)} %param.9), calls=%async_computation.7 | async-start | bytes 1024 | tf_op jit(solution)/shard_map/dynamic_slice | solution.py:12
  234.1 163.3 %copy-start = (f32[2,2048,64]{1,0,2:T(2,128)S(1)}, f32[2,2048,64]{1,0,2:T(2,128)}, u32[]{:S(2)}) copy-start(f32[2,2048,64]{1,0,2:T(2,128)} %slice.148) | copy-start | bytes 3145732
  353.2 53.6 %copy-start.3 = (f32[2048]{0:T(1024)S(1)}, f32[2048]{0:T(1024)}, u32[]{:S(2)}) copy-start(f32[2048]{0:T(1024)} %param.9) | copy-start | bytes 24580
  353.2 53.7 %slice-start = ((f32[2048,256]{1,0:T(8,128)}), f32[64,256]{1,0:T(8,128)S(1)}, s32[]{:S(2)}) async-start(f32[2048,256]{1,0:T(8,128)} %param.10), calls=%async_computation.6 | async-start | bytes 131072 | tf_op jit(solution)/shard_map/slice | solution.py:58
  354.8 101.4 %all-gather.5.cloned.1.call-start = ((), (), s32[]{:S(2)}) async-start(), calls=%async_computation.4 | async-start | bytes 1179648 | tf_op jit(solution)/shard_map/all_gather | solution.py:57
  401.6 47.4 %all-to-all-start = ((f32[8,1,32768]{2,1,0:T(1,128)}), f32[8,1,32768]{2,1,0:T(1,128)S(1)}, u32[]{:S(2)}, u32[]{:S(2)}) async-start(f32[8,1,32768]{2,1,0:T(1,128)} %reshape.114), calls=%async_computation.1 | async-start | bytes 2097152 | tf_op jit(solution)/shard_map/all_to_all | solution.py:47
  406.2 192.7 %reduce-scatter.2.cloned.1.call-start = ((), (), s32[]{:S(2)}) async-start(), calls=%async_computation.5 | async-start | bytes 5242880 | tf_op jit(solution)/shard_map/reduce_scatter | solution.py:49
  454.1 136.3 %copy-start.1 = (f32[512,256]{1,0:T(8,128)S(1)}, f32[512,256]{1,0:T(8,128)}, u32[]{:S(2)}) copy-start(f32[512,256]{1,0:T(8,128)} %all_gather.11) | copy-start | bytes 1572868
Sparse Core Ops, SparseCore 0:
  145.0 84.7 all-gather.2
  354.9 40.6 all-reduce.3
  397.9 27.8 all-gather.4
  428.5 56.0 reduce-scatter.1
where the time goes:
time: 614 us; the launch traced here: 609 us
  other arithmetic  163 us (27%)
  matrix products  133 us (22%)
  waiting for transfers between devices  126 us (21%)
  local copies, waits for them, and re-layouts  123 us (20%)
  blocking collectives  42.1 us (7%)
  between operations  17 us (3%)
    dot_general x1, matrix products, per_device(): lax.dot_general(flat_masked, scaled, (((0,), (0,)), ((), ())), precision=...  119 us
    all_gather x1, waiting for transfers between devices, per_device(): shard_cols = lax.all_gather(own_panel, 'col', axis=2, tiled=True)  84.8 us
    another operation x14, other arithmetic, per_device(): factor = jnp.linalg.cholesky(pivot_block)  78.7 us
    unnamed x12, local copies, waits for them, and re-layouts  54 us
    mul x2, local copies, waits for them, and re-layouts, per_device(): masked = (masked * weights).reshape(scen_local, row_total, own_width)  51.8 us
    all_gather x1, blocking collectives, per_device(): lax.all_gather(rhs[:pivot_width], 'col', axis=0, tiled=True)  42.1 us
    psum x1, waiting for transfers between devices, per_device(): pivot_summed = lax.psum(schur_term[:pivot_width], 'scen')  40.8 us
    another operation x4, other arithmetic, per_device(): lax.linalg.triangular_solve(factor, rhs_panel, left_side=True, lower=True)  39.5 us
  transfers between devices with their start and end apart: 5, of which 2 were waited for; matrix products, arithmetic and copies ran while one was open for 25% of the time, Pallas kernels for 0%

commit v1 on v0

v1 whole, which is shorter than its diff:
```python
import functools

import jax
import jax.numpy as jnp
from jax import lax
from jax.experimental import pallas as pl
from jax.experimental.pallas import tpu as pltpu
from jax.sharding import PartitionSpec as P

PW = 512
BLK = 128
HIGHEST = lax.Precision.HIGHEST


def dot(a, b, contract=((1,), (0,))):
    return lax.dot_general(
        a, b, (contract, ((), ())), precision=HIGHEST, preferred_element_type=jnp.float32
    )


def invert_factor(block):
    groups = BLK // 8
    shape = (8, BLK)
    sub = lax.broadcasted_iota(jnp.int32, shape, 0)
    lane = lax.broadcasted_iota(jnp.int32, shape, 1)
    rows = [block[8 * i : 8 * i + 8, :] for i in range(groups)]
    inverse = [jnp.where(lane == sub + 8 * i, 1.0, 0.0).astype(jnp.float32) for i in range(groups)]
    for g in range(groups):
        columns = [
            {i: jnp.broadcast_to(rows[i][:, 8 * g + m : 8 * g + m + 1], shape) for i in range(g, groups)}
            for m in range(8)
        ]
        pivots = jnp.ones(shape, jnp.float32)
        for m in range(8):
            head = columns[m][g]
            pivot = jnp.broadcast_to(head[m : m + 1, :], shape)
            scale = 1.0 / pivot
            pivots = jnp.where(sub == m, pivot, pivots)
            row = jnp.broadcast_to(rows[g][m : m + 1, :], shape) * scale
            inverse_row = jnp.broadcast_to(inverse[g][m : m + 1, :], shape) * scale
            factors = [
                jnp.broadcast_to(head[later : later + 1, :], shape) * scale for later in range(m + 1, 8)
            ]
            for i in range(g, groups):
                column = columns[m][i]
                if i == g:
                    column = jnp.where(sub > m, column, 0.0)
                rows[i] = rows[i] - column * row
                inverse[i] = inverse[i] - column * inverse_row
                for later in range(m + 1, 8):
                    columns[later][i] = columns[later][i] - column * factors[later - m - 1]
        inverse[g] = inverse[g] * lax.rsqrt(pivots)
    return jnp.concatenate(inverse, axis=0)


def solve_kernel(packed, rhs, forward, solved, matrix, right, upper, inverses):
    steps = matrix.shape[0] // BLK
    matrix[...] = jnp.zeros_like(matrix)
    offset = 0
    for i in range(steps):
        width = matrix.shape[1] - i * BLK
        matrix[i * BLK : (i + 1) * BLK, i * BLK :] = packed[:, offset : offset + width]
        offset += width
    right[...] = rhs[...]
    solved[...] = jnp.zeros_like(solved)

    def eliminate(j, carry):
        here = pl.ds(pl.multiple_of(j * BLK, BLK), BLK)
        inverse = invert_factor(matrix[here, here])
        inverses[here, :] = inverse
        wide = dot(inverse, matrix[here, :])
        part = dot(inverse, right[here, :])
        cols = lax.broadcasted_iota(jnp.int32, wide.shape, 1)
        wide = jnp.where(cols >= (j + 1) * BLK, wide, 0.0)
        upper[here, :] = wide
        forward[here, :] = part
        matrix[...] -= dot(wide, wide, ((0,), (0,)))
        right[...] -= dot(wide, part, ((0,), (0,)))
        return carry

    lax.fori_loop(0, steps, eliminate, 0)

    def substitute(t, carry):
        here = pl.ds(pl.multiple_of((steps - 1 - t) * BLK, BLK), BLK)
        rest = forward[here, :] - dot(upper[here, :], solved[...])
        solved[here, :] = dot(inverses[here, :], rest, ((0,), (0,)))
        return carry

    lax.fori_loop(0, steps, substitute, 0)


def factor_and_solve(packed, rhs):
    size, width = rhs.shape
    out = jax.ShapeDtypeStruct((size, width), jnp.float32)
    return pl.pallas_call(
        solve_kernel,
        out_shape=(out, out),
        in_specs=[pl.BlockSpec(memory_space=pltpu.VMEM)] * 2,
        out_specs=[pl.BlockSpec(memory_space=pltpu.VMEM)] * 2,
        scratch_shapes=[
            pltpu.VMEM((size, size), jnp.float32),
            pltpu.VMEM((size, width), jnp.float32),
            pltpu.VMEM((size, size), jnp.float32),
            pltpu.VMEM((size, BLK), jnp.float32),
        ],
    )(packed, rhs)


def halves(x):
    high = x.astype(jnp.bfloat16)
    return high, (x - high.astype(jnp.float32)).astype(jnp.bfloat16)


def apply_kernel(row_block, border, mask, weights, out, total):
    step = pl.program_id(0) * pl.num_programs(1) + pl.program_id(1)
    last = pl.num_programs(0) * pl.num_programs(1) - 1

    @pl.when(step == 0)
    def _():
        total[...] = jnp.zeros_like(total)

    blocks = [
        border[0, r * row_block : (r + 1) * row_block, :] * mask[0, r] for r in range(mask.shape[1])
    ]
    high, low = halves(jnp.concatenate(blocks, axis=0) if len(blocks) > 1 else blocks[0])
    w_high, w_low = halves(weights[0, 0])
    count = w_high.shape[0]
    both = jnp.dot(
        jnp.concatenate([w_high, w_low], axis=0), high, preferred_element_type=jnp.float32
    )
    total[...] += both[:count] + both[count:] + jnp.dot(w_high, low, preferred_element_type=jnp.float32)

    @pl.when(step == last)
    def _():
        share = out.shape[2]
        for d in range(out.shape[0]):
            out[d] = total[:, d * share : (d + 1) * share]


def apply_border(border, mask, weights, parts):
    scen_local, row_total, own_width = border.shape
    col_count, _, rhs_count, row_share = weights.shape
    row_block = row_total // mask.shape[1]
    per_step = row_share // row_block
    return pl.pallas_call(
        functools.partial(apply_kernel, row_block),
        grid=(scen_local, col_count),
        in_specs=[
            pl.BlockSpec((1, row_share, own_width), lambda s, c: (s, c, 0)),
            pl.BlockSpec((1, per_step, 1, own_width), lambda s, c: (s, c, 0, 0)),
            pl.BlockSpec((1, 1, rhs_count, row_share), lambda s, c: (c, s, 0, 0)),
        ],
        out_specs=pl.BlockSpec((parts, rhs_count, own_width // parts), lambda s, c: (0, 0, 0)),
        out_shape=jax.ShapeDtypeStruct((parts, rhs_count, own_width // parts), jnp.float32),
        scratch_shapes=[pltpu.VMEM((rhs_count, own_width), jnp.float32)],
        compiler_params=pltpu.CompilerParams(vmem_limit_bytes=40 << 20),
    )(border, mask, weights)


def per_device(border, pattern, slack, first_diag, rhs, scen_rhs):
    col_count = lax.axis_size("col")
    scen_count = lax.axis_size("scen")
    col_index = lax.axis_index("col")
    scen_index = lax.axis_index("scen")
    scen_local, row_total, own_width = border.shape
    row_blocks, width_blocks = pattern.shape[1:]
    row_block = row_total // row_blocks
    col_block = own_width // width_blocks
    pivot_width = PW // col_count
    row_share = row_total // col_count
    own_share = own_width // scen_count

    rhs_panel = lax.all_gather(rhs[:pivot_width], "col", axis=0, tiled=True)
    weights = pattern.astype(jnp.float32)
    row_weights = jnp.repeat(weights, row_block, axis=1)
    panel_weights = jnp.repeat(row_weights[:, :, : -(-pivot_width // col_block)], col_block, axis=2)
    own_panel = border[:, :, :pivot_width] * panel_weights[:, :, :pivot_width]
    sent = own_panel.reshape(scen_local, col_count, row_share, pivot_width).transpose(1, 0, 3, 2)
    got = lax.all_to_all(sent, "col", split_axis=0, concat_axis=0, tiled=True)
    panel = got.transpose(1, 0, 2, 3).reshape(scen_local, PW, row_share)

    slack_rows = lax.dynamic_slice_in_dim(slack, col_index * row_share, row_share, 1)
    inverse_slack = 1.0 / slack_rows
    gram = lax.dot_general(
        panel * inverse_slack[:, None, :],
        panel,
        (((0, 2), (0, 2)), ((), ())),
        precision=HIGHEST,
        preferred_element_type=jnp.float32,
    )
    order = jnp.arange(PW, dtype=jnp.int32)
    mine = (order // pivot_width == col_index) & (scen_index == 0)
    diagonal = jnp.where(mine, jnp.tile(first_diag[:pivot_width], col_count), 0.0)
    gram = gram + jnp.where(order[:, None] == order[None, :], diagonal[:, None], 0.0)
    packed = jnp.concatenate(
        [gram[i * BLK : (i + 1) * BLK, i * BLK :] for i in range(PW // BLK)], axis=1
    )
    packed = lax.psum(packed, ("scen", "col"))
    forward, solved = factor_and_solve(packed, rhs_panel)

    moved = lax.dot_general(
        solved,
        panel,
        (((0,), (1,)), ((), ())),
        precision=HIGHEST,
        preferred_element_type=jnp.float32,
    ).transpose(1, 0, 2)
    scaled = moved * inverse_slack[:, None, :]
    everyone = lax.all_gather(scaled, "col", axis=0)
    mask = jnp.repeat(weights, col_block, axis=2)[:, :, None, :]
    terms = apply_border(border, mask, everyone, scen_count)
    summed = lax.psum_scatter(terms, "scen", scatter_dimension=0, tiled=True)[0]

    directions = (scen_rhs - moved.transpose(0, 2, 1)) / slack_rows[:, :, None]
    row_start = scen_index * own_share
    rhs_rows = lax.dynamic_slice_in_dim(rhs, row_start, own_share)
    reduced = rhs_rows - summed.T
    own_forward = lax.dynamic_slice_in_dim(forward, col_index * pivot_width, pivot_width)
    padded = jnp.pad(own_forward, ((0, own_width - pivot_width), (0, 0)))
    placed = lax.dynamic_slice_in_dim(padded, row_start, own_share)
    local_rows = row_start + jnp.arange(own_share, dtype=jnp.int32)
    reduced = jnp.where((local_rows < pivot_width)[:, None], placed, reduced)
    return reduced[None], directions


def solution(mesh):
    return jax.shard_map(
        per_device,
        mesh=mesh,
        in_specs=(
            P("scen", None, "col"),
            P("scen", None, "col"),
            P("scen", None),
            P("col"),
            P("col", None),
            P("scen", "col", None),
        ),
        out_specs=(P("col", "scen", None), P("scen", "col", None)),
        check_vma=False,
    )
```

time: 614 us -> 325 us (0.53)
  other arithmetic: 163 us -> 6.16 us
  matrix products: 133 us -> 3.96 us
  local copies, waits for them, and re-layouts: 123 us -> 7.74 us
  waiting for transfers between devices: 126 us -> 217 us
  Pallas kernels: 0 us -> 53.8 us
  blocking collectives: 42.1 us -> 16 us
    dot_general x3 -> x2, matrix products: 126 us -> 3.96 us  [the longest x1 2.1 us: per_device(): lax.dot_general(solved, panel, (((0,), (1,)), ((), ())), precision=HIGHES...]
    another operation x18 -> x0, other arithmetic: 118 us -> none  [the longest x14 78.7 us: per_device(): factor = jnp.linalg.cholesky(pivot_block)]
    psum x1, waiting for transfers between devices: 40.8 us -> 113 us  [per_device(): packed = lax.psum(packed, ('scen', 'col'))]
    pallas_call x0 -> x2, Pallas kernels: none -> 53.8 us  [the longest x1 29.3 us: factor_and_solve(): pl.pallas_call(solve_kernel, out_shape=(out, out), in_specs=[pl.BlockSpec...]
    mul x2 -> x0, local copies, waits for them, and re-layouts: 51.8 us -> none  [per_device(): masked = (masked * weights).reshape(scen_local, row_total, own_width)]
    unnamed x12 -> x8, local copies, waits for them, and re-layouts: 54 us -> 3.39 us
    all_gather x2 -> x1, waiting for transfers between devices: 84.8 us -> 46 us  [per_device(): everyone = lax.all_gather(scaled, 'col', axis=0)]
    mul x2 -> x3, other arithmetic: 37.5 us -> 2.89 us  [the longest x1 1.98 us: per_device(): own_panel = border[:, :, :pivot_width] * panel_weights[:, :, :pivot_width]]
  transfers between devices with their start and end apart: 5 -> 4, of which waited for: 2 -> 4; matrix products, arithmetic and copies ran while one was open for 25% -> 1% of each run, Pallas kernels for 0% -> 0%
where the time goes in v1:
time: 325 us
  waiting for transfers between devices  217 us (67%)
  Pallas kernels  53.8 us (17%)
  blocking collectives  16 us (5%)
  between operations  14 us (4%)
  local copies, waits for them, and re-layouts  7.74 us (2%)
  starting transfers between devices  6.47 us (2%)
  other arithmetic  6.16 us (2%)
  matrix products  3.96 us (1%)
    psum x1, waiting for transfers between devices, per_device(): packed = lax.psum(packed, ('scen', 'col'))  113 us
    all_gather x1, waiting for transfers between devices, per_device(): everyone = lax.all_gather(scaled, 'col', axis=0)  46 us
    unnamed x4, waiting for transfers between devices  32.3 us
    pallas_call x1, Pallas kernels, factor_and_solve(): pl.pallas_call(solve_kernel, out_shape=(out, out), in_specs=[pl.BlockSpec...  29.3 us
    all_to_all x1, waiting for transfers between devices, per_device(): got = lax.all_to_all(sent, 'col', split_axis=0, concat_axis=0, tiled=True)  25.7 us
    pallas_call x1, Pallas kernels, apply_border(): pl.pallas_call(functools.partial(apply_kernel, row_block), grid=(scen_loc...  24.5 us
    all_gather x1, blocking collectives, per_device(): rhs_panel = lax.all_gather(rhs[:pivot_width], 'col', axis=0, tiled=True)  16 us
  transfers between devices with their start and end apart: 4, of which 4 were waited for; matrix products, arithmetic and copies ran while one was open for 1% of the time, Pallas kernels for 0%

profile of v1, /device:TPU:0, one launch (start us, length us, event | category | flops | bytes accessed | tf_op | source)
XLA Modules:
  0.0 324.7 jit_solution(879909937764977779)
XLA Ops:
  7.2 0.7 convert_element_type.5
  7.9 0.1 copy.24
  8.0 0.1 broadcast_in_dim.42
  8.1 0.1 reshape.44
  8.3 2.0 slice_multiply_fusion
  10.3 1.6 copy.26
  11.8 6.4 %all-to-all-start = ((f32[8,2,64,256]{3,2,1,0:T(8,128)}), f32[8,2,64,256]{3,2,1,0:T(8,128)S(1)}, u32[]{:S(2)}, u32[]{:S(2)}) async-start(f32[8,2,64,256]{3,2,1,0:T(8,128)} %copy.26), calls=%async_computation | async-start | bytes 2097152 | tf_op jit(solution)/shard_map/all_to_all | solution.py:179
  18.2 0.0 all-reduce.4.cloned.1.call-start
  18.2 0.1 tile.10
  18.3 0.7 broadcast_divide_fusion
  19.0 25.7 %all-to-all-done = f32[8,2,64,256]{3,2,1,0:T(8,128)S(1)} async-done(((f32[8,2,64,256]{3,2,1,0:T(8,128)}), f32[8,2,64,256]{3,2,1,0:T(8,128)S(1)}, u32[]{:S(2)}, u32[]{:S(2)}) %all-to-all-start) | async-done | bytes 1048608 | tf_op jit(solution)/shard_map/all_to_all | solution.py:179
  44.7 0.1 copy.27
  44.8 0.1 bitcast_multiply_fusion
  44.9 1.9 fusion
  46.9 0.9 pad_maximum_fusion
  47.8 0.0 all-gather.3.cloned.1.call-start
  47.9 0.2 copy.31
  48.1 16.0 %all_gather.9.rhs = f32[512,256]{1,0:T(8,128)} all-gather(f32[64,256]{1,0:T(8,128)S(1)} %slice-done), channel_id=1, replica_groups=mesh['scen'=4,'col'=8] {'col'}, dimensions={0}, use_global_device_ids=true | all-gather | bytes 589824 | tf_op jit(solution)/shard_map/all_gather | solution.py:173
  64.1 112.6 %all-reduce.4.cloned.1.call-done.packed = f32[128,1280]{1,0:T(8,128)} async-done(((f32[128,1280]{1,0:T(8,128)}), f32[128,1280]{1,0:T(8,128)}) %all-reduce.4.cloned.1.call-update) | async-done | bytes 655376 | tf_op jit(solution)/shard_map/psum | solution.py:198
  176.7 29.3 %shard_map.77 = (f32[512,256]{1,0:T(8,128)}, f32[512,256]{1,0:T(8,128)}) custom-call(f32[128,1280]{1,0:T(8,128)} %all-reduce.4.cloned.1.call-done.packed, f32[512,256]{1,0:T(8,128)} %all_gather.9.rhs), custom_call_target="tpu_custom_call" | custom-call | tf_op jit(solution)/shard_map/pallas_call | solution.py:95
  206.0 2.1 fusion.3
  208.1 0.8 multiply_bitcast_fusion
  208.9 0.0 reduce-scatter.4.cloned.1.call-start
  209.0 46.0 %all-gather.3.cloned.1.call-done = f32[16,256,256]{2,1,0:T(8,128)} async-done(((f32[2,256,256]{2,1,0:T(8,128)}), f32[16,256,256]{2,1,0:T(8,128)}) %all-gather.3.cloned.1.call-update) | async-done | bytes 4194320 | tf_op jit(solution)/shard_map/all_gather | solution.py:209
  255.0 0.1 broadcast_in_dim.46
  255.1 2.2 copy-done
  257.3 24.5 %shard_map.78 = f32[4,256,512]{2,1,0:T(8,128)} custom-call(f32[2,2048,2048]{2,1,0:T(8,128)} %border.1, f32[2,16,1,2048]{3,2,1,0:T(1,128)S(1)} %bitcast.45, f32[8,2,256,256]{3,2,1,0:T(8,128)S(1)} %bitcast.44), custom_call_target="tpu_custom_call" | custom-call | tf_op jit(solution)/shard_map/pallas_call | solution.py:145
  281.9 1.0 copy.32
  282.9 0.8 constant_dynamic-slice_fusion
  283.7 32.3 %reduce-scatter.4.cloned.1.call-done = f32[1,256,512]{2,1,0:T(8,128)} async-done(((f32[4,256,512]{2,1,0:T(8,128)}), f32[1,256,512]{2,1,0:T(8,128)}) %reduce-scatter.4.cloned.1.call-update) | async-done | bytes 524304
  316.0 1.2 copy.30
  317.2 0.9 fusion.2
  (20 shorter events, 0.2 us)
Async XLA Ops:
  10.2 8.0 %slice-start.1 = ((f32[2048]{0:T(1024)}), f32[64]{0:T(128)S(1)}, s32[]{:S(2)}) async-start(f32[2048]{0:T(1024)} %param.9), calls=%async_computation.6 | async-start | bytes 1024 | tf_op jit(solution)/shard_map/slice | solution.py:193
  11.8 32.9 %all-to-all-start = ((f32[8,2,64,256]{3,2,1,0:T(8,128)}), f32[8,2,64,256]{3,2,1,0:T(8,128)S(1)}, u32[]{:S(2)}, u32[]{:S(2)}) async-start(f32[8,2,64,256]{3,2,1,0:T(8,128)} %copy.26), calls=%async_computation | async-start | bytes 2097152 | tf_op jit(solution)/shard_map/all_to_all | solution.py:179
  18.2 158.5 %all-reduce.4.cloned.1.call-start = ((), (), s32[]{:S(2)}) async-start(), calls=%async_computation.2 | async-start | bytes 1310720 | tf_op jit(solution)/shard_map/psum | solution.py:198
  46.8 1.1 copy-start.1
  46.8 1.3 slice-start
  47.8 207.1 %all-gather.3.cloned.1.call-start = ((), (), s32[]{:S(2)}) async-start(), calls=%async_computation.3 | async-start | bytes 4718592 | tf_op jit(solution)/shard_map/all_gather | solution.py:209
  208.9 107.0 %reduce-scatter.4.cloned.1.call-start = ((), (), s32[]{:S(2)}) async-start(), calls=%async_computation.4 | async-start | bytes 2621440
  255.1 2.2 copy-start
  281.8 35.4 %copy-start.2 = (f32[2048,256]{1,0:T(8,128)S(1)}, f32[2048,256]{1,0:T(8,128)}, u32[]{:S(2)}) copy-start(f32[2048,256]{1,0:T(8,128)} %param.10) | copy-start | bytes 6291460
Sparse Core Ops, SparseCore 0:
  48.0 128.6 all-reduce.3
  209.0 45.8 all-gather.2
  282.0 33.9 reduce-scatter.3

commit v2 on v1

--- a/solution.py
+++ b/solution.py
@@ -111,9 +111,9 @@
     return high, (x - high.astype(jnp.float32)).astype(jnp.bfloat16)
 
 
-def apply_kernel(row_block, border, mask, weights, out, total):
-    step = pl.program_id(0) * pl.num_programs(1) + pl.program_id(1)
-    last = pl.num_programs(0) * pl.num_programs(1) - 1
+def apply_kernel(row_block, border, mask, weights, *rest):
+    before, (out, total) = rest[:-2], rest[-2:]
+    step = pl.program_id(0)
 
     @pl.when(step == 0)
     def _():
@@ -123,38 +123,46 @@
         border[0, r * row_block : (r + 1) * row_block, :] * mask[0, r] for r in range(mask.shape[1])
     ]
     high, low = halves(jnp.concatenate(blocks, axis=0) if len(blocks) > 1 else blocks[0])
-    w_high, w_low = halves(weights[0, 0])
+    w_high, w_low = halves(weights[0])
     count = w_high.shape[0]
     both = jnp.dot(
         jnp.concatenate([w_high, w_low], axis=0), high, preferred_element_type=jnp.float32
     )
     total[...] += both[:count] + both[count:] + jnp.dot(w_high, low, preferred_element_type=jnp.float32)
 
-    @pl.when(step == last)
+    @pl.when(step == pl.num_programs(0) - 1)
     def _():
         share = out.shape[2]
         for d in range(out.shape[0]):
-            out[d] = total[:, d * share : (d + 1) * share]
-
-
-def apply_border(border, mask, weights, parts):
-    scen_local, row_total, own_width = border.shape
-    col_count, _, rhs_count, row_share = weights.shape
+            value = total[:, d * share : (d + 1) * share]
+            out[d] = value + before[0][d] if before else value
+
+
+def apply_border(border, mask, weights, scenario, parts, before):
+    _, row_total, own_width = border.shape
+    col_count, rhs_count, row_share = weights.shape
     row_block = row_total // mask.shape[1]
     per_step = row_share // row_block
+    whole = (parts, rhs_count, own_width // parts)
     return pl.pallas_call(
         functools.partial(apply_kernel, row_block),
-        grid=(scen_local, col_count),
+        grid=(col_count,),
         in_specs=[
-            pl.BlockSpec((1, row_share, own_width), lambda s, c: (s, c, 0)),
-            pl.BlockSpec((1, per_step, 1, own_width), lambda s, c: (s, c, 0, 0)),
-            pl.BlockSpec((1, 1, rhs_count, row_share), lambda s, c: (c, s, 0, 0)),
-        ],
-        out_specs=pl.BlockSpec((parts, rhs_count, own_width // parts), lambda s, c: (0, 0, 0)),
-        out_shape=jax.ShapeDtypeStruct((parts, rhs_count, own_width // parts), jnp.float32),
+            pl.BlockSpec((1, row_share, own_width), lambda c: (scenario, c, 0)),
+            pl.BlockSpec((1, per_step, 1, own_width), lambda c: (scenario, c, 0, 0)),
+            pl.BlockSpec((1, rhs_count, row_share), lambda c: (c, 0, 0)),
+        ]
+        + [pl.BlockSpec(whole, lambda c: (0, 0, 0)) for _ in before],
+        out_specs=pl.BlockSpec(whole, lambda c: (0, 0, 0)),
+        out_shape=jax.ShapeDtypeStruct(whole, jnp.float32),
         scratch_shapes=[pltpu.VMEM((rhs_count, own_width), jnp.float32)],
         compiler_params=pltpu.CompilerParams(vmem_limit_bytes=40 << 20),
-    )(border, mask, weights)
+        cost_estimate=pl.CostEstimate(
+            flops=6 * row_total * own_width * rhs_count,
+            bytes_accessed=4 * row_total * own_width,
+            transcendentals=0,
+        ),
+    )(border, mask, weights, *before)
 
 
 def per_device(border, pattern, slack, first_diag, rhs, scen_rhs):
@@ -170,7 +178,6 @@
     row_share = row_total // col_count
     own_share = own_width // scen_count
 
-    rhs_panel = lax.all_gather(rhs[:pivot_width], "col", axis=0, tiled=True)
     weights = pattern.astype(jnp.float32)
     row_weights = jnp.repeat(weights, row_block, axis=1)
     panel_weights = jnp.repeat(row_weights[:, :, : -(-pivot_width // col_block)], col_block, axis=2)
@@ -195,8 +202,12 @@
     packed = jnp.concatenate(
         [gram[i * BLK : (i + 1) * BLK, i * BLK :] for i in range(PW // BLK)], axis=1
     )
-    packed = lax.psum(packed, ("scen", "col"))
-    forward, solved = factor_and_solve(packed, rhs_panel)
+    piece = lax.psum_scatter(packed, "col", scatter_dimension=0, tiled=True)
+    piece = lax.psum(piece, "scen")
+    own_rhs = rhs[:pivot_width].reshape(piece.shape[0], -1)
+    joined = lax.all_gather(jnp.concatenate([piece, own_rhs], axis=1), "col", axis=0, tiled=True)
+    rhs_panel = joined[:, packed.shape[1] :].reshape(PW, rhs.shape[1])
+    forward, solved = factor_and_solve(joined[:, : packed.shape[1]], rhs_panel)
 
     moved = lax.dot_general(
         solved,
@@ -206,9 +217,12 @@
         preferred_element_type=jnp.float32,
     ).transpose(1, 0, 2)
     scaled = moved * inverse_slack[:, None, :]
-    everyone = lax.all_gather(scaled, "col", axis=0)
     mask = jnp.repeat(weights, col_block, axis=2)[:, :, None, :]
-    terms = apply_border(border, mask, everyone, scen_count)
+    terms = ()
+    for scenario in range(scen_local):
+        everyone = lax.all_gather(scaled[scenario], "col", axis=0)
+        terms = (apply_border(border, mask, everyone, scenario, scen_count, terms),)
+    terms = terms[0]
     summed = lax.psum_scatter(terms, "scen", scatter_dimension=0, tiled=True)[0]
 
     directions = (scen_rhs - moved.transpose(0, 2, 1)) / slack_rows[:, :, None]

time: 325 us -> 302 us (0.929)
  waiting for transfers between devices: 217 us -> 200 us
  blocking collectives: 16 us -> 0 us
  local copies, waits for them, and re-layouts: 7.74 us -> 14 us
    psum x1, waiting for transfers between devices: 113 us -> 42.4 us  [per_device(): piece = lax.psum(piece, 'scen')]
    reduce_scatter x0 -> x1, waiting for transfers between devices: none -> 30.7 us  [per_device(): piece = lax.psum_scatter(packed, 'col', scatter_dimension=0, tiled=True)]
    all_gather x1 -> x3, waiting for transfers between devices: 46 us -> 68 us  [the longest x2 44 us: per_device(): everyone = lax.all_gather(scaled[scenario], 'col', axis=0)]
    all_gather x1 -> x0, blocking collectives: 16 us -> none  [per_device(): rhs_panel = lax.all_gather(rhs[:pivot_width], 'col', axis=0, tiled=True)]
    unnamed x4 -> x7, waiting for transfers between devices: 32.3 us -> 33.5 us
    pallas_call x1 -> x2, Pallas kernels: 24.5 us -> 24.7 us  [apply_border(): pl.pallas_call(functools.partial(apply_kernel, row_block), grid=(col_coun...]
  transfers between devices with their start and end apart: 4 -> 7, of which waited for: 4 -> 7; matrix products, arithmetic and copies ran while one was open for 1% -> 1% of each run, Pallas kernels for 0% -> 4%
where the time goes in v2:
time: 302 us; the launch traced here: 301 us
  waiting for transfers between devices  200 us (66%)
  Pallas kernels  54 us (18%)
  between operations  14.4 us (5%)
  local copies, waits for them, and re-layouts  14 us (5%)
  other arithmetic  7.96 us (3%)
  starting transfers between devices  6.77 us (2%)
  matrix products  3.96 us (1%)
    all_gather x2, waiting for transfers between devices, per_device(): everyone = lax.all_gather(scaled[scenario], 'col', axis=0)  44 us
    psum x1, waiting for transfers between devices, per_device(): piece = lax.psum(piece, 'scen')  42.4 us
    unnamed x7, waiting for transfers between devices  33.5 us
    reduce_scatter x1, waiting for transfers between devices, per_device(): piece = lax.psum_scatter(packed, 'col', scatter_dimension=0, tiled=True)  30.7 us
    pallas_call x1, Pallas kernels, factor_and_solve(): pl.pallas_call(solve_kernel, out_shape=(out, out), in_specs=[pl.BlockSpec...  29.3 us
    all_to_all x1, waiting for transfers between devices, per_device(): got = lax.all_to_all(sent, 'col', split_axis=0, concat_axis=0, tiled=True)  25.7 us
    pallas_call x2, Pallas kernels, apply_border(): pl.pallas_call(functools.partial(apply_kernel, row_block), grid=(col_coun...  24.7 us
    all_gather x1, waiting for transfers between devices, per_device(): lax.all_gather(jnp.concatenate([piece, own_rhs], axis=1), 'col', axis=0,...  23.9 us
  transfers between devices with their start and end apart: 7, of which 7 were waited for; matrix products, arithmetic and copies ran while one was open for 1% of the time, Pallas kernels for 4%

profile of v2, /device:TPU:0, one launch (start us, length us, event | category | flops | bytes accessed | tf_op | source)
XLA Modules:
  0.0 301.3 jit_solution(6153738852399001021)
XLA Ops:
  7.2 0.7 convert_element_type.5
  8.3 2.0 slice_multiply_fusion
  10.3 1.6 copy.26
  11.8 6.4 %all-to-all-start = ((f32[8,2,64,256]{3,2,1,0:T(8,128)}), f32[8,2,64,256]{3,2,1,0:T(8,128)S(1)}, u32[]{:S(2)}, u32[]{:S(2)}) async-start(f32[8,2,64,256]{3,2,1,0:T(8,128)} %copy.26), calls=%async_computation | async-start | bytes 2097152 | tf_op jit(solution)/shard_map/all_to_all | solution.py:186
  18.3 0.7 broadcast_divide_fusion
  19.0 25.7 %all-to-all-done = f32[8,2,64,256]{3,2,1,0:T(8,128)S(1)} async-done(((f32[8,2,64,256]{3,2,1,0:T(8,128)}), f32[8,2,64,256]{3,2,1,0:T(8,128)S(1)}, u32[]{:S(2)}, u32[]{:S(2)}) %all-to-all-start) | async-done | bytes 1048608 | tf_op jit(solution)/shard_map/all_to_all | solution.py:186
  44.9 1.9 fusion
  46.9 0.9 pad_maximum_fusion
  47.9 30.7 %reduce-scatter.5.cloned.1.call-done = f32[16,1280]{1,0:T(8,128)} async-done(((f32[128,1280]{1,0:T(8,128)}), f32[16,1280]{1,0:T(8,128)}) %reduce-scatter.5.cloned.1.call-update) | async-done | bytes 81936 | tf_op jit(solution)/shard_map/reduce_scatter | solution.py:205
  78.7 42.4 %all-reduce.4.cloned.1.call-done = f32[16,1280]{1,0:T(8,128)} async-done(((f32[16,1280]{1,0:T(8,128)}), f32[16,1280]{1,0:T(8,128)}) %all-reduce.4.cloned.1.call-update) | async-done | bytes 81936 | tf_op jit(solution)/shard_map/psum | solution.py:206
  121.1 1.6 pad_maximum_fusion.1
  122.9 23.9 %all-gather.4.cloned.1.call-done = f32[128,2304]{1,0:T(8,128)} async-done(((f32[16,2304]{1,0:T(8,128)}), f32[128,2304]{1,0:T(8,128)}) %all-gather.4.cloned.1.call-update) | async-done | bytes 1179664 | tf_op jit(solution)/shard_map/all_gather | solution.py:208
  146.8 1.2 slice.61
  148.0 0.9 reshape.54.rhs
  149.0 0.9 slice.60.packed
  149.9 29.3 %shard_map.77 = (f32[512,256]{1,0:T(8,128)}, f32[512,256]{1,0:T(8,128)}) custom-call(f32[128,1280]{1,0:T(8,128)} %slice.60.packed, f32[512,256]{1,0:T(8,128)} %reshape.54.rhs), custom_call_target="tpu_custom_call" | custom-call | tf_op jit(solution)/shard_map/pallas_call | solution.py:95
  179.2 2.1 fusion.3
  181.3 0.8 fusion.12
  182.2 0.5 all-gather.6.cloned.1.call-update
  182.8 0.2 reduce-scatter.7.cloned.1.call-start
  183.0 28.1 %all-gather.8.cloned.1.call-done.weights = f32[8,256,256]{2,1,0:T(8,128)} async-done(((f32[1,256,256]{2,1,0:T(8,128)}), f32[8,256,256]{2,1,0:T(8,128)}) %all-gather.8.cloned.1.call-update) | async-done | bytes 2097168 | tf_op jit(solution)/shard_map/all_gather | solution.py:223
  211.3 1.6 copy-done.1
  212.9 12.4 %shard_map.78.rest_0_ = f32[4,256,512]{2,1,0:T(8,128)S(1)} custom-call(f32[2,2048,2048]{2,1,0:T(8,128)} %border.3, f32[2,16,1,2048]{3,2,1,0:T(1,128)S(1)} %bitcast.43, f32[8,256,256]{2,1,0:T(8,128)S(1)} %copy-done.1), custom_call_target="tpu_custom_call" | custom-call | flops 6442450944 | bytes 16777216 | tf_op jit(solution)/shard_map/pallas_call | solution.py:147
  225.3 15.9 %all-gather.6.cloned.1.call-done.weights = f32[8,256,256]{2,1,0:T(8,128)} async-done(((f32[1,256,256]{2,1,0:T(8,128)}), f32[8,256,256]{2,1,0:T(8,128)}) %all-gather.6.cloned.1.call-update) | async-done | bytes 2097168 | tf_op jit(solution)/shard_map/all_gather | solution.py:223
  241.2 1.6 copy-done.2
  242.8 12.3 %shard_map.79 = f32[4,256,512]{2,1,0:T(8,128)S(1)} custom-call(f32[2,2048,2048]{2,1,0:T(8,128)} %border.3, f32[2,16,1,2048]{3,2,1,0:T(1,128)S(1)} %bitcast.44, f32[8,256,256]{2,1,0:T(8,128)S(1)} %copy-done.2, f32[4,256,512]{2,1,0:T(8,128)S(1)} %shard_map.78.rest_0_), custom_call_target="tpu_custom_call" | custom-call | flops 6442450944 | bytes 16777216 | tf_op jit(solution)/shard_map/pallas_call | solution.py:147
  255.1 1.3 copy-done
  256.5 1.0 copy.32
  257.5 0.8 constant_dynamic-slice_fusion
  258.3 32.9 %reduce-scatter.7.cloned.1.call-done = f32[1,256,512]{2,1,0:T(8,128)} async-done(((f32[4,256,512]{2,1,0:T(8,128)}), f32[1,256,512]{2,1,0:T(8,128)}) %reduce-scatter.7.cloned.1.call-update) | async-done | bytes 524304
  291.2 1.2 copy.30
  292.4 2.0 fusion.2
  (39 shorter events, 1.4 us)
Async XLA Ops:
  10.2 8.0 %slice-start.1 = ((f32[2048]{0:T(1024)}), f32[64]{0:T(128)S(1)}, s32[]{:S(2)}) async-start(f32[2048]{0:T(1024)} %param.9), calls=%async_computation.10 | async-start | bytes 1024 | tf_op jit(solution)/shard_map/slice | solution.py:200
  11.8 32.9 %all-to-all-start = ((f32[8,2,64,256]{3,2,1,0:T(8,128)}), f32[8,2,64,256]{3,2,1,0:T(8,128)S(1)}, u32[]{:S(2)}, u32[]{:S(2)}) async-start(f32[8,2,64,256]{3,2,1,0:T(8,128)} %copy.26), calls=%async_computation | async-start | bytes 2097152 | tf_op jit(solution)/shard_map/all_to_all | solution.py:186
  18.2 60.4 %reduce-scatter.5.cloned.1.call-start = ((), (), s32[]{:S(2)}) async-start(), calls=%async_computation.3 | async-start | bytes 737280 | tf_op jit(solution)/shard_map/reduce_scatter | solution.py:205
  46.8 31.8 %slice-start = ((f32[2048,256]{1,0:T(8,128)}), f32[64,256]{1,0:T(8,128)S(1)}, s32[]{:S(2)}) async-start(f32[2048,256]{1,0:T(8,128)} %param.10), calls=%async_computation.9 | async-start | bytes 131072 | tf_op jit(solution)/shard_map/slice | solution.py:207
  46.8 75.9 %copy-start.4 = (f32[2,256,256]{2,1,0:T(8,128)S(1)}, f32[2,256,256]{2,1,0:T(8,128)}, u32[]{:S(2)}) copy-start(f32[2,256,256]{2,1,0:T(8,128)} %param.11) | copy-start | bytes 1572868
  47.9 73.2 %all-reduce.4.cloned.1.call-start = ((), (), s32[]{:S(2)}) async-start(), calls=%async_computation.4 | async-start | bytes 163840 | tf_op jit(solution)/shard_map/psum | solution.py:206
  78.6 68.3 %all-gather.4.cloned.1.call-start = ((), (), s32[]{:S(2)}) async-start(), calls=%async_computation.5 | async-start | bytes 1327104 | tf_op jit(solution)/shard_map/all_gather | solution.py:208
  122.7 88.5 %all-gather.8.cloned.1.call-start = ((), (), s32[]{:S(2)}) async-start(), calls=%async_computation.7 | async-start | bytes 2359296 | tf_op jit(solution)/shard_map/all_gather | solution.py:223
  146.8 2.1 copy-start.3
  182.2 59.0 %all-gather.6.cloned.1.call-start = ((), (), s32[]{:S(2)}) async-start(), calls=%async_computation.6 | async-start | bytes 2359296 | tf_op jit(solution)/shard_map/all_gather | solution.py:223
  182.8 108.4 %reduce-scatter.7.cloned.1.call-start = ((), (), s32[]{:S(2)}) async-start(), calls=%async_computation.8 | async-start | bytes 2621440
  211.3 1.6 copy-start.1
  241.2 1.6 copy-start.2
  255.1 1.3 copy-start
Sparse Core Ops, SparseCore 0:
  48.0 30.5 reduce-scatter.4
  81.5 39.5 all-reduce.3
  123.3 23.5 all-gather.3
  182.3 28.7 all-gather.7
  212.6 28.5 all-gather.5
  256.6 34.5 reduce-scatter.6

commit v3 on v2

--- a/solution.py
+++ b/solution.py
@@ -202,8 +202,10 @@
     packed = jnp.concatenate(
         [gram[i * BLK : (i + 1) * BLK, i * BLK :] for i in range(PW // BLK)], axis=1
     )
-    piece = lax.psum_scatter(packed, "col", scatter_dimension=0, tiled=True)
-    piece = lax.psum(piece, "scen")
+    pieces = lax.all_to_all(
+        packed.reshape(col_count, -1, packed.shape[1]), "col", split_axis=0, concat_axis=0, tiled=True
+    )
+    piece = lax.all_gather(jnp.sum(pieces, axis=0), "scen", axis=0).sum(axis=0)
     own_rhs = rhs[:pivot_width].reshape(piece.shape[0], -1)
     joined = lax.all_gather(jnp.concatenate([piece, own_rhs], axis=1), "col", axis=0, tiled=True)
     rhs_panel = joined[:, packed.shape[1] :].reshape(PW, rhs.shape[1])
@@ -223,7 +225,7 @@
         everyone = lax.all_gather(scaled[scenario], "col", axis=0)
         terms = (apply_border(border, mask, everyone, scenario, scen_count, terms),)
     terms = terms[0]
-    summed = lax.psum_scatter(terms, "scen", scatter_dimension=0, tiled=True)[0]
+    summed = lax.all_to_all(terms, "scen", split_axis=0, concat_axis=0, tiled=True).sum(axis=0)
 
     directions = (scen_rhs - moved.transpose(0, 2, 1)) / slack_rows[:, :, None]
     row_start = scen_index * own_share

time: 302 us -> 250 us (0.83)
  waiting for transfers between devices: 200 us -> 133 us
  blocking collectives: 0 us -> 9.25 us
  starting transfers between devices: 6.77 us -> 14 us
    psum x1 -> x0, waiting for transfers between devices: 42.4 us -> none  [per_device(): piece = lax.psum(piece, 'scen')]
    all_to_all x0 -> x2, waiting for transfers between devices: none -> 41.6 us  [the longest x1 23.6 us: per_device(): lax.all_to_all(terms, 'scen', split_axis=0, concat_axis=0, tiled=True)]
    unnamed x7 -> x3, waiting for transfers between devices: 33.5 us -> 0.53 us
    reduce_scatter x1 -> x0, waiting for transfers between devices: 30.7 us -> none  [per_device(): piece = lax.psum_scatter(packed, 'col', scatter_dimension=0, tiled=True)]
    all_gather x0 -> x1, blocking collectives: none -> 9.25 us  [per_device(): piece = lax.all_gather(jnp.sum(pieces, axis=0), 'scen', axis=0).sum(axis=0)]
    all_to_all x0 -> x2, starting transfers between devices: none -> 7.31 us  [the longest x1 3.67 us: per_device(): lax.all_to_all(packed.reshape(col_count, -1, packed.shape[1]), 'col', spl...]
    all_gather x1, waiting for transfers between devices: 23.9 us -> 20.6 us  [per_device(): lax.all_gather(jnp.concatenate([piece, own_rhs], axis=1), 'col', axis=0,...]
  transfers between devices with their start and end apart: 7 -> 6, of which waited for: 7 -> 6; matrix products, arithmetic and copies ran while one was open for 1% -> 1% of each run, Pallas kernels for 4% -> 5%
where the time goes in v3:
time: 250 us; the launch traced here: 249 us
  waiting for transfers between devices  133 us (53%)
  Pallas kernels  54 us (22%)
  local copies, waits for them, and re-layouts  14 us (6%)
  starting transfers between devices  14 us (6%)
  between operations  14 us (6%)
  blocking collectives  9.25 us (4%)
  other arithmetic  6.51 us (3%)
  matrix products  3.96 us (2%)
    all_gather x2, waiting for transfers between devices, per_device(): everyone = lax.all_gather(scaled[scenario], 'col', axis=0)  44.3 us
    pallas_call x1, Pallas kernels, factor_and_solve(): pl.pallas_call(solve_kernel, out_shape=(out, out), in_specs=[pl.BlockSpec...  29.3 us
    all_to_all x1, waiting for transfers between devices, per_device(): got = lax.all_to_all(sent, 'col', split_axis=0, concat_axis=0, tiled=True)  25.8 us
    pallas_call x2, Pallas kernels, apply_border(): pl.pallas_call(functools.partial(apply_kernel, row_block), grid=(col_coun...  24.8 us
    all_to_all x1, waiting for transfers between devices, per_device(): lax.all_to_all(terms, 'scen', split_axis=0, concat_axis=0, tiled=True)  23.6 us
    all_gather x1, waiting for transfers between devices, per_device(): lax.all_gather(jnp.concatenate([piece, own_rhs], axis=1), 'col', axis=0,...  20.6 us
    all_to_all x1, waiting for transfers between devices, per_device(): lax.all_to_all(packed.reshape(col_count, -1, packed.shape[1]), 'col', spl...  18 us
    all_gather x1, blocking collectives, per_device(): piece = lax.all_gather(jnp.sum(pieces, axis=0), 'scen', axis=0).sum(axis=0)  9.25 us
  transfers between devices with their start and end apart: 6, of which 6 were waited for; matrix products, arithmetic and copies ran while one was open for 1% of the time, Pallas kernels for 5%

profile of v3, /device:TPU:0, one launch (start us, length us, event | category | flops | bytes accessed | tf_op | source)
XLA Modules:
  0.0 248.6 jit_solution(7727357415558736910)
XLA Ops:
  7.2 0.7 convert_element_type.5
  8.3 2.0 slice_multiply_fusion
  10.3 1.6 copy.37
  11.8 6.4 %all-to-all-start = ((f32[8,2,64,256]{3,2,1,0:T(8,128)}), f32[8,2,64,256]{3,2,1,0:T(8,128)S(1)}, u32[]{:S(2)}, u32[]{:S(2)}) async-start(f32[8,2,64,256]{3,2,1,0:T(8,128)} %copy.37), calls=%async_computation | async-start | bytes 2097152 | tf_op jit(solution)/shard_map/all_to_all | solution.py:186
  18.3 0.7 broadcast_divide_fusion
  19.0 25.8 %all-to-all-done = f32[8,2,64,256]{3,2,1,0:T(8,128)S(1)} async-done(((f32[8,2,64,256]{3,2,1,0:T(8,128)}), f32[8,2,64,256]{3,2,1,0:T(8,128)S(1)}, u32[]{:S(2)}, u32[]{:S(2)}) %all-to-all-start) | async-done | bytes 1048608 | tf_op jit(solution)/shard_map/all_to_all | solution.py:186
  44.9 1.9 fusion
  47.0 1.1 copy.39
  48.1 3.7 %all-to-all-start.1 = ((f32[8,16,1280]{2,1,0:T(8,128)}), f32[8,16,1280]{2,1,0:T(8,128)S(1)}, u32[]{:S(2)}, u32[]{:S(2)}) async-start(f32[8,16,1280]{2,1,0:T(8,128)} %bitcast.8), calls=%async_computation.1 | async-start | bytes 1310720 | tf_op jit(solution)/shard_map/all_to_all | solution.py:205
  51.8 18.0 %all-to-all-done.1 = f32[8,16,1280]{2,1,0:T(8,128)S(1)} async-done(((f32[8,16,1280]{2,1,0:T(8,128)}), f32[8,16,1280]{2,1,0:T(8,128)S(1)}, u32[]{:S(2)}, u32[]{:S(2)}) %all-to-all-start.1) | async-done | bytes 655392 | tf_op jit(solution)/shard_map/all_to_all | solution.py:205
  69.9 9.3 %all-gather = f32[64,1280]{1,0:T(8,128)S(1)} all-gather(f32[16,1280]{1,0:T(8,128)S(1)} %reduce_sum.27), channel_id=2, replica_groups=mesh['scen'=4,'col'=8] {'scen'}, dimensions={0}, use_global_device_ids=true | all-gather | bytes 409600 | tf_op jit(solution)/shard_map/all_gather | solution.py:208
  79.1 0.7 pad_maximum_fusion.1
  80.1 20.6 %all-gather.5.cloned.1.call-done = f32[128,2304]{1,0:T(8,128)} async-done(((f32[16,2304]{1,0:T(8,128)}), f32[128,2304]{1,0:T(8,128)}) %all-gather.5.cloned.1.call-update) | async-done | bytes 1179664 | tf_op jit(solution)/shard_map/all_gather | solution.py:210
  100.7 1.2 slice.61
  101.9 0.9 reshape.58.rhs
  102.8 0.9 slice.60.packed
  103.7 29.3 %shard_map.77 = (f32[512,256]{1,0:T(8,128)}, f32[512,256]{1,0:T(8,128)}) custom-call(f32[128,1280]{1,0:T(8,128)} %slice.60.packed, f32[512,256]{1,0:T(8,128)} %reshape.58.rhs), custom_call_target="tpu_custom_call" | custom-call | tf_op jit(solution)/shard_map/pallas_call | solution.py:95
  133.0 2.1 fusion.3
  135.2 0.8 fusion.12
  136.3 0.5 all-gather.7.cloned.1.call-update
  136.8 28.2 %all-gather.9.cloned.1.call-done.weights = f32[8,256,256]{2,1,0:T(8,128)} async-done(((f32[1,256,256]{2,1,0:T(8,128)}), f32[8,256,256]{2,1,0:T(8,128)}) %all-gather.9.cloned.1.call-update) | async-done | bytes 2097168 | tf_op jit(solution)/shard_map/all_gather | solution.py:225
  165.1 1.6 copy-done.1
  166.7 12.4 %shard_map.78.rest_0_ = f32[4,256,512]{2,1,0:T(8,128)S(1)} custom-call(f32[2,2048,2048]{2,1,0:T(8,128)} %border.3, f32[2,16,1,2048]{3,2,1,0:T(1,128)S(1)} %bitcast.42, f32[8,256,256]{2,1,0:T(8,128)S(1)} %copy-done.1), custom_call_target="tpu_custom_call" | custom-call | flops 6442450944 | bytes 16777216 | tf_op jit(solution)/shard_map/pallas_call | solution.py:147
  179.2 16.1 %all-gather.7.cloned.1.call-done.weights = f32[8,256,256]{2,1,0:T(8,128)} async-done(((f32[1,256,256]{2,1,0:T(8,128)}), f32[8,256,256]{2,1,0:T(8,128)}) %all-gather.7.cloned.1.call-update) | async-done | bytes 2097168 | tf_op jit(solution)/shard_map/all_gather | solution.py:225
  195.2 1.6 copy-done.2
  196.8 12.3 %shard_map.79 = f32[4,256,512]{2,1,0:T(8,128)S(1)} custom-call(f32[2,2048,2048]{2,1,0:T(8,128)} %border.3, f32[2,16,1,2048]{3,2,1,0:T(1,128)S(1)} %bitcast.43, f32[8,256,256]{2,1,0:T(8,128)S(1)} %copy-done.2, f32[4,256,512]{2,1,0:T(8,128)S(1)} %shard_map.78.rest_0_), custom_call_target="tpu_custom_call" | custom-call | flops 6442450944 | bytes 16777216 | tf_op jit(solution)/shard_map/pallas_call | solution.py:147
  209.1 1.3 copy-done
  210.5 3.6 %all-to-all-start.2 = ((f32[4,256,512]{2,1,0:T(8,128)}), f32[4,256,512]{2,1,0:T(8,128)S(1)}, u32[]{:S(2)}, u32[]{:S(2)}) async-start(f32[4,256,512]{2,1,0:T(8,128)} %copy-done), calls=%async_computation.2 | async-start | bytes 4194304 | tf_op jit(solution)/shard_map/all_to_all | solution.py:228
  214.1 1.0 copy.43
  215.1 0.8 constant_dynamic-slice_fusion
  216.0 23.6 %all-to-all-done.2 = f32[4,256,512]{2,1,0:T(8,128)S(1)} async-done(((f32[4,256,512]{2,1,0:T(8,128)}), f32[4,256,512]{2,1,0:T(8,128)S(1)}, u32[]{:S(2)}, u32[]{:S(2)}) %all-to-all-start.2) | async-done | bytes 2097184 | tf_op jit(solution)/shard_map/all_to_all | solution.py:228
  240.0 2.0 fusion.2
  (39 shorter events, 2.0 us)
Async XLA Ops:
  10.2 7.9 %slice-start.1 = ((f32[2048]{0:T(1024)}), f32[64]{0:T(128)S(1)}, s32[]{:S(2)}) async-start(f32[2048]{0:T(1024)} %param.9), calls=%async_computation.7 | async-start | bytes 1024 | tf_op jit(solution)/shard_map/slice | solution.py:200
  11.8 32.9 %all-to-all-start = ((f32[8,2,64,256]{3,2,1,0:T(8,128)}), f32[8,2,64,256]{3,2,1,0:T(8,128)S(1)}, u32[]{:S(2)}, u32[]{:S(2)}) async-start(f32[8,2,64,256]{3,2,1,0:T(8,128)} %copy.37), calls=%async_computation | async-start | bytes 2097152 | tf_op jit(solution)/shard_map/all_to_all | solution.py:186
  46.9 4.9 %slice-start = ((f32[2048,256]{1,0:T(8,128)}), f32[64,256]{1,0:T(8,128)S(1)}, s32[]{:S(2)}) async-start(f32[2048,256]{1,0:T(8,128)} %param.10), calls=%async_computation.6 | async-start | bytes 131072 | tf_op jit(solution)/shard_map/slice | solution.py:209
  48.1 31.8 %copy-start.4 = (f32[2,256,256]{2,1,0:T(8,128)S(1)}, f32[2,256,256]{2,1,0:T(8,128)}, u32[]{:S(2)}) copy-start(f32[2,256,256]{2,1,0:T(8,128)} %param.11) | copy-start | bytes 1572868
  48.1 21.7 %all-to-all-start.1 = ((f32[8,16,1280]{2,1,0:T(8,128)}), f32[8,16,1280]{2,1,0:T(8,128)S(1)}, u32[]{:S(2)}, u32[]{:S(2)}) async-start(f32[8,16,1280]{2,1,0:T(8,128)} %bitcast.8), calls=%async_computation.1 | async-start | bytes 1310720 | tf_op jit(solution)/shard_map/all_to_all | solution.py:205
  51.8 49.0 %all-gather.5.cloned.1.call-start = ((), (), s32[]{:S(2)}) async-start(), calls=%async_computation.3 | async-start | bytes 1327104 | tf_op jit(solution)/shard_map/all_gather | solution.py:210
  79.8 85.2 %all-gather.9.cloned.1.call-start = ((), (), s32[]{:S(2)}) async-start(), calls=%async_computation.5 | async-start | bytes 2359296 | tf_op jit(solution)/shard_map/all_gather | solution.py:225
  100.7 2.1 copy-start.3
  136.0 59.2 %all-gather.7.cloned.1.call-start = ((), (), s32[]{:S(2)}) async-start(), calls=%async_computation.4 | async-start | bytes 2359296 | tf_op jit(solution)/shard_map/all_gather | solution.py:225
  165.1 1.6 copy-start.1
  195.2 1.6 copy-start.2
  209.1 1.3 copy-start
  210.5 29.1 %all-to-all-start.2 = ((f32[4,256,512]{2,1,0:T(8,128)}), f32[4,256,512]{2,1,0:T(8,128)S(1)}, u32[]{:S(2)}, u32[]{:S(2)}) async-start(f32[4,256,512]{2,1,0:T(8,128)} %copy-done), calls=%async_computation.2 | async-start | bytes 4194304 | tf_op jit(solution)/shard_map/all_to_all | solution.py:228
Sparse Core Ops, SparseCore 0:
  80.0 20.7 all-gather.4
  136.2 28.7 all-gather.8
  166.6 28.5 all-gather.6
